TPU v7x, 32 devices: a whole 2x2x4 slice. The times are simulated.
32 devices in a mesh: energy: 8 (over y, x, core), section: 4 (over z).
Axes of the slice: x: 2, y: 2, z: 4, core: 2. Of those that a mesh axis runs over, the one named last changes fastest.
Arguments:
- self_in: float32 [32, 4, 2, 256, 256], P('energy', 'section'), as said below
- onsite: float32 [4, 256], P('section'), may hold values from -1 to 1
- within: float32 [4, 256, 256], P('section'), may hold values from -0.09375 to 0.09375
- between: float32 [4, 256, 256], P('section'), as said below
- coupling: float32 [4, 256, 256], P('section'), may hold values from -1 to 1
- groups: int32 [4, 256], P('section'), may hold values from 0 to 3
- offsets: int32 [3], replicated, may hold values from 1 to 2, as said below
- strength: float32 [3], replicated, may hold values from 0.3 to 1
Outputs:
- green: float32 [32, 4, 2, 256, 256], P('energy', 'section')
- self_out: float32 [32, 4, 2, 256, 256], P('energy', 'section')
Inputs may be any that keep to these rules, and one draw needn't show every extreme that they name: `offsets`: every entry lies between 1 and 2, and one entry equals 2. `self_in`: imaginary parts of diagonal entries lie between -0.02 and -0.002, real parts of diagonal entries between -0.3 and 0.3; off-diagonal entries lie between -0.01 and 0.01. `between`: diagonal entries lie between 1.4 and 2.0; off-diagonal entries are at most 1.12 / sqrt(256) in magnitude.
All inputs are finite; a program needn't handle non-finite values.
Results may differ from a plain program's by a relative error of at most 0.0001.
Values sent between devices are 32-bit elements; how exact they have to be, the bound alone decides.
A program may use at most 128 MiB of HBM per device.

v0:
```python
import jax
import jax.numpy as jnp
from jax import lax
from jax.sharding import PartitionSpec as P

NEWTON = 3
MODES = 3


HIGH = lax.Precision.HIGHEST
ETA = 1.0
CONTACT = 0.6


def passed_along(value, axis, steps):
    count = lax.axis_size(axis)
    initial, last = (max(0, -steps), min(count, count - steps))
    return lax.ppermute(value, axis, [(source, source + steps) for source in range(initial, last)])


def padded(block, sides, width):
    for axis, dim in sides:
        count = lax.axis_size(axis)
        forward = [(i, i + 1) for i in range(count - 1)]
        backward = [(target, source) for source, target in forward]
        low = lax.ppermute(
            lax.slice_in_dim(block, block.shape[dim] - width, None, axis=dim), axis, forward
        )
        high = lax.ppermute(lax.slice_in_dim(block, 0, width, axis=dim), axis, backward)
        block = jnp.concatenate([low, block, high], axis=dim)
    return block


def multiply(left, right):
    return jnp.einsum("...ij,...jk->...ik", left, right, precision=HIGH)


def product(left, right):
    real_a, imag_a = (left[..., 0, :, :], left[..., 1, :, :])
    real_b, imag_b = (right[..., 0, :, :], right[..., 1, :, :])
    return jnp.stack(
        [
            multiply(real_a, real_b) - multiply(imag_a, imag_b),
            multiply(real_a, imag_b) + multiply(imag_a, real_b),
        ],
        axis=-3,
    )


def times_real(field, matrix):
    return jnp.einsum("...ij,jk->...ik", field, matrix, precision=HIGH)


def real_times(matrix, field):
    return jnp.einsum("ij,...jk->...ik", matrix, field, precision=HIGH)


def newton(system):
    sys_re, sys_im = (system[..., 0, :, :], system[..., 1, :, :])
    real_c = jnp.diagonal(sys_re, axis1=-2, axis2=-1)
    imag_c = jnp.diagonal(sys_im, axis1=-2, axis2=-1)
    modulus = real_c * real_c + imag_c * imag_c
    inv_re = real_c / modulus
    inv_im = -imag_c / modulus
    half_re = inv_re[..., :, None] * sys_re - inv_im[..., :, None] * sys_im
    half_im = inv_re[..., :, None] * sys_im + inv_im[..., :, None] * sys_re
    full_re = half_re * inv_re[..., None, :] - half_im * inv_im[..., None, :]
    full_im = half_re * inv_im[..., None, :] + half_im * inv_re[..., None, :]
    identity = jnp.eye(system.shape[-1], dtype=jnp.float32)
    iterate = jnp.stack(
        [
            2.0 * inv_re[..., :, None] * identity - full_re,
            2.0 * inv_im[..., :, None] * identity - full_im,
        ],
        axis=-3,
    )
    for sweep in range(NEWTON - 1):
        iterate = 2.0 * iterate - product(iterate, product(system, iterate))
    return iterate


def local_inverse(energy, hamil, sigma, previous, hop):
    identity = jnp.eye(hamil.shape[-1], dtype=jnp.float32)
    left = real_times(hop.T, times_real(previous, hop))
    sys_re = energy[..., None, None] * identity - hamil - sigma[..., 0, :, :] - left[..., 0, :, :]
    sys_im = ETA * identity - sigma[..., 1, :, :] - left[..., 1, :, :]
    return newton(jnp.stack([sys_re, sys_im], axis=-3))


def refine(local_green, incoming):
    return local_green + product(local_green, product(incoming, local_green))


def sandwich(hop, green):
    return times_real(real_times(hop, green), hop.T)


def forward_pass(energy_part, sigma_part, previous, hams, between):

    def advance(carried, items):
        hamil, hop, sigma = items
        local_green = local_inverse(energy_part, hamil, sigma, carried, hop)
        return (local_green, local_green)

    _, pieces = lax.scan(advance, previous, (hams, between, jnp.swapaxes(sigma_part, 0, 1)))
    return jnp.swapaxes(pieces, 0, 1)


def backward_pass(locals_part, incoming, between):

    def retreat(carried, items):
        local_green, hop = items
        full = refine(local_green, carried)
        return (sandwich(hop, full), full)

    sent, greens = lax.scan(
        retreat, incoming, (jnp.swapaxes(locals_part, 0, 1), between), reverse=True
    )
    return (jnp.swapaxes(greens, 0, 1), sent)


def per_device(self_in, onsite, within, between, coupling, groups, offsets, strength):
    e_dev, s_dev, width = (self_in.shape[0], self_in.shape[1], self_in.shape[3])
    identity = jnp.eye(width, dtype=jnp.float32)
    hams = onsite[:, :, None] * identity + 0.5 * (within + jnp.swapaxes(within, 1, 2))
    sections = lax.axis_size("section")
    place = lax.axis_index("section")
    total = e_dev * lax.axis_size("energy")
    first_index = lax.axis_index("energy") * e_dev
    energies = (
        -1.0
        + (2 * (first_index + jnp.arange(e_dev, dtype=jnp.int32)) + 1).astype(jnp.float32) / total
    )
    batch = 1
    rounds = e_dev // batch
    contact = jnp.broadcast_to(
        jnp.stack([jnp.zeros((width, width), jnp.float32), -CONTACT * identity]),
        (batch, 2, width, width),
    )
    message = jnp.zeros((batch, 2, width, width), jnp.float32)
    store = jnp.zeros_like(self_in)

    def forward_segment(segment, carry):
        locals_all, outgoing = carry
        received = passed_along(outgoing, "section", 1)
        turn = segment - place
        valid = (turn >= 0) & (turn < rounds)
        start = jnp.clip(turn, 0, rounds - 1) * batch
        previous = jnp.where(place == 0, contact, received)

        def forward_work(unused):
            energy_part = lax.dynamic_slice_in_dim(energies, start, batch, 0)
            sigma_part = lax.dynamic_slice_in_dim(self_in, start, batch, 0)
            pieces = forward_pass(energy_part, sigma_part, previous, hams, between)
            return (lax.dynamic_update_slice_in_dim(locals_all, pieces, start, 0), pieces[:, -1])

        def forward_skip(unused):
            return (locals_all, jnp.zeros_like(outgoing))

        return lax.cond(valid, forward_work, forward_skip, None)

    locals_all, _ = lax.fori_loop(0, sections + rounds - 1, forward_segment, (store, message))

    def backward_segment(segment, carry):
        greens_all, outgoing = carry
        received = passed_along(outgoing, "section", -1)
        turn = segment - (sections - 1 - place)
        valid = (turn >= 0) & (turn < rounds)
        start = jnp.clip(turn, 0, rounds - 1) * batch

        def backward_work(unused):
            locals_part = lax.dynamic_slice_in_dim(locals_all, start, batch, 0)
            pieces, sent = backward_pass(locals_part, received, between)
            return (lax.dynamic_update_slice_in_dim(greens_all, pieces, start, 0), sent)

        def backward_skip(unused):
            return (greens_all, jnp.zeros_like(outgoing))

        return lax.cond(valid, backward_work, backward_skip, None)

    green, _ = lax.fori_loop(0, sections + rounds - 1, backward_segment, (store, message))
    extended = padded(green, (("energy", 0),), e_dev)
    summed = jnp.zeros_like(green)
    for mode in range(MODES):
        shift = offsets[mode]
        lower = lax.dynamic_slice_in_dim(extended, e_dev - shift, e_dev, 0)
        upper = lax.dynamic_slice_in_dim(extended, e_dev + shift, e_dev, 0)
        summed = summed + strength[mode] * (lower + upper)
    mats = jnp.where(groups[:, :, None] == groups[:, None, :], coupling, jnp.float32(0.0))
    first_half = jnp.einsum("sab,eszbc->eszac", mats, summed, precision=HIGH)
    self_out = jnp.einsum("eszac,sdc->eszad", first_half, mats, precision=HIGH)
    return (green, self_out)


def solution(mesh):
    placed = (
        P("energy", "section", None, None, None),
        P("section", None),
        P("section", None, None),
        P("section", None, None),
        P("section", None, None),
        P("section", None),
        P(),
        P(),
    )
    return jax.shard_map(
        per_device,
        mesh=mesh,
        in_specs=placed,
        out_specs=(
            P("energy", "section", None, None, None),
            P("energy", "section", None, None, None),
        ),
        check_vma=False,
    )
```

profile of v0, /device:TPU:4, one launch (start us, length us, event | category | flops | bytes accessed | tf_op | source)
XLA Modules:
  0.0 439.9 jit_solution(9283429669535805337)
XLA Ops:
  6.4 201.0 %while.51 = (s32[]{:T(128)}, f32[4,1,2,256,256]{3,4,2,1,0:T(8,128)}, f32[1,2,256,256]{2,3,1,0:T(8,128)}, s32[]{:T(128)}, f32[1,256,256]{1,2,0:T(8,128)S(1)}, /*i...) while((s32[]{:T(128)}, ...), condition=%wide.region_3.4_spmd.clone, body=%wide.region_0.3_spmd.clone.sunk | while | flops 4031646720 | bytes 31741320 | solution.py:162
  11.2 11.1 %collective-permute-done.1 = f32[1,2,256,256]{3,2,1,0:T(8,128)S(1)} collective-permute-done((f32[1,2,256,256]{3,2,1,0:T(8,128)S(1)}, f32[1,2,256,256]{3,2,1,0:T(8,128)S(1)}, u32[]{:S(2)}, u32[]{:S(2)}) %collective-permute-start.1) | collective-permute-done | bytes 524320 | tf_op jit(solution)/shard_map/while/body/eval_jaxpr/ppermute | solution.py:18
  22.3 20.3 %conditional.6 = (f32[4,1,2,256,256]{3,4,2,1,0:T(8,128)}, f32[1,2,256,256]{2,3,1,0:T(8,128)}) conditional(s32[]{:T(128)} %convert_element_type.85, f32[4,1,2,256,256]{3,4,2,1,0:T(8,128)} %get-tuple-element.749, (s32[]{:T(128)}, f32[4]{0:T(128)S(1)}, f32[1,256,256]{1,2,0:T(8,128)S(1)}, f32[4,1,2,256,256]{3,4,2,1,0:T(8,128)}, pred[]{:T(512)}, ...), branch_computations={%region_1.1_spmd, %region_2.2_spmd.clone} | conditional | flops 4031646720 | bytes 28595296 | solution.py:160
  45.2 10.5 %collective-permute-done.1 = f32[1,2,256,256]{3,2,1,0:T(8,128)S(1)} collective-permute-done((f32[1,2,256,256]{3,2,1,0:T(8,128)S(1)}, f32[1,2,256,256]{3,2,1,0:T(8,128)S(1)}, u32[]{:S(2)}, u32[]{:S(2)}) %collective-permute-start.1) | collective-permute-done | bytes 524320 | tf_op jit(solution)/shard_map/while/body/eval_jaxpr/ppermute | solution.py:18
  55.7 20.3 %conditional.6 = (f32[4,1,2,256,256]{3,4,2,1,0:T(8,128)}, f32[1,2,256,256]{2,3,1,0:T(8,128)}) conditional(s32[]{:T(128)} %convert_element_type.85, f32[4,1,2,256,256]{3,4,2,1,0:T(8,128)} %get-tuple-element.749, (s32[]{:T(128)}, f32[4]{0:T(128)S(1)}, f32[1,256,256]{1,2,0:T(8,128)S(1)}, f32[4,1,2,256,256]{3,4,2,1,0:T(8,128)}, pred[]{:T(512)}, ...), branch_computations={%region_1.1_spmd, %region_2.2_spmd.clone} | conditional | flops 4031646720 | bytes 28595296 | solution.py:160
  77.3 4.4 %collective-permute-start.1 = (f32[1,2,256,256]{3,2,1,0:T(8,128)S(1)}, f32[1,2,256,256]{3,2,1,0:T(8,128)S(1)}, u32[]{:S(2)}, u32[]{:S(2)}) collective-permute-start(f32[1,2,256,256]{3,2,1,0:T(8,128)S(1)} %copy.65), channel_id=1, source_target_pairs={{0,1},{1,2},{2,3},{4,5},{5,6},{6,7},{8,9},{9,10},{10,11},{12,13},{... | collective-permute-start | bytes 1572872 | tf_op jit(solution)/shard_map/while/body/eval_jaxpr/ppermute | solution.py:18
  81.8 9.7 %collective-permute-done.1 = f32[1,2,256,256]{3,2,1,0:T(8,128)S(1)} collective-permute-done((f32[1,2,256,256]{3,2,1,0:T(8,128)S(1)}, f32[1,2,256,256]{3,2,1,0:T(8,128)S(1)}, u32[]{:S(2)}, u32[]{:S(2)}) %collective-permute-start.1) | collective-permute-done | bytes 524320 | tf_op jit(solution)/shard_map/while/body/eval_jaxpr/ppermute | solution.py:18
  91.4 20.3 %conditional.6 = (f32[4,1,2,256,256]{3,4,2,1,0:T(8,128)}, f32[1,2,256,256]{2,3,1,0:T(8,128)}) conditional(s32[]{:T(128)} %convert_element_type.85, f32[4,1,2,256,256]{3,4,2,1,0:T(8,128)} %get-tuple-element.749, (s32[]{:T(128)}, f32[4]{0:T(128)S(1)}, f32[1,256,256]{1,2,0:T(8,128)S(1)}, f32[4,1,2,256,256]{3,4,2,1,0:T(8,128)}, pred[]{:T(512)}, ...), branch_computations={%region_1.1_spmd, %region_2.2_spmd.clone} | conditional | flops 4031646720 | bytes 28595296 | solution.py:160
  113.0 4.4 %collective-permute-start.1 = (f32[1,2,256,256]{3,2,1,0:T(8,128)S(1)}, f32[1,2,256,256]{3,2,1,0:T(8,128)S(1)}, u32[]{:S(2)}, u32[]{:S(2)}) collective-permute-start(f32[1,2,256,256]{3,2,1,0:T(8,128)S(1)} %copy.65), channel_id=1, source_target_pairs={{0,1},{1,2},{2,3},{4,5},{5,6},{6,7},{8,9},{9,10},{10,11},{12,13},{... | collective-permute-start | bytes 1572872 | tf_op jit(solution)/shard_map/while/body/eval_jaxpr/ppermute | solution.py:18
  117.5 8.8 %collective-permute-done.1 = f32[1,2,256,256]{3,2,1,0:T(8,128)S(1)} collective-permute-done((f32[1,2,256,256]{3,2,1,0:T(8,128)S(1)}, f32[1,2,256,256]{3,2,1,0:T(8,128)S(1)}, u32[]{:S(2)}, u32[]{:S(2)}) %collective-permute-start.1) | collective-permute-done | bytes 524320 | tf_op jit(solution)/shard_map/while/body/eval_jaxpr/ppermute | solution.py:18
  126.3 20.3 %conditional.6 = (f32[4,1,2,256,256]{3,4,2,1,0:T(8,128)}, f32[1,2,256,256]{2,3,1,0:T(8,128)}) conditional(s32[]{:T(128)} %convert_element_type.85, f32[4,1,2,256,256]{3,4,2,1,0:T(8,128)} %get-tuple-element.749, (s32[]{:T(128)}, f32[4]{0:T(128)S(1)}, f32[1,256,256]{1,2,0:T(8,128)S(1)}, f32[4,1,2,256,256]{3,4,2,1,0:T(8,128)}, pred[]{:T(512)}, ...), branch_computations={%region_1.1_spmd, %region_2.2_spmd.clone} | conditional | flops 4031646720 | bytes 28595296 | solution.py:160
  147.8 4.4 %collective-permute-start.1 = (f32[1,2,256,256]{3,2,1,0:T(8,128)S(1)}, f32[1,2,256,256]{3,2,1,0:T(8,128)S(1)}, u32[]{:S(2)}, u32[]{:S(2)}) collective-permute-start(f32[1,2,256,256]{3,2,1,0:T(8,128)S(1)} %copy.65), channel_id=1, source_target_pairs={{0,1},{1,2},{2,3},{4,5},{5,6},{6,7},{8,9},{9,10},{10,11},{12,13},{... | collective-permute-start | bytes 1572872 | tf_op jit(solution)/shard_map/while/body/eval_jaxpr/ppermute | solution.py:18
  152.3 8.0 %collective-permute-done.1 = f32[1,2,256,256]{3,2,1,0:T(8,128)S(1)} collective-permute-done((f32[1,2,256,256]{3,2,1,0:T(8,128)S(1)}, f32[1,2,256,256]{3,2,1,0:T(8,128)S(1)}, u32[]{:S(2)}, u32[]{:S(2)}) %collective-permute-start.1) | collective-permute-done | bytes 524320 | tf_op jit(solution)/shard_map/while/body/eval_jaxpr/ppermute | solution.py:18
  162.3 23.9 %collective-permute-start.1 = (f32[1,2,256,256]{3,2,1,0:T(8,128)S(1)}, f32[1,2,256,256]{3,2,1,0:T(8,128)S(1)}, u32[]{:S(2)}, u32[]{:S(2)}) collective-permute-start(f32[1,2,256,256]{3,2,1,0:T(8,128)S(1)} %copy.65), channel_id=1, source_target_pairs={{0,1},{1,2},{2,3},{4,5},{5,6},{6,7},{8,9},{9,10},{10,11},{12,13},{... | collective-permute-start | bytes 1572872 | tf_op jit(solution)/shard_map/while/body/eval_jaxpr/ppermute | solution.py:18
  186.2 7.1 %collective-permute-done.1 = f32[1,2,256,256]{3,2,1,0:T(8,128)S(1)} collective-permute-done((f32[1,2,256,256]{3,2,1,0:T(8,128)S(1)}, f32[1,2,256,256]{3,2,1,0:T(8,128)S(1)}, u32[]{:S(2)}, u32[]{:S(2)}) %collective-permute-start.1) | collective-permute-done | bytes 524320 | tf_op jit(solution)/shard_map/while/body/eval_jaxpr/ppermute | solution.py:18
  195.4 4.4 %collective-permute-start.1 = (f32[1,2,256,256]{3,2,1,0:T(8,128)S(1)}, f32[1,2,256,256]{3,2,1,0:T(8,128)S(1)}, u32[]{:S(2)}, u32[]{:S(2)}) collective-permute-start(f32[1,2,256,256]{3,2,1,0:T(8,128)S(1)} %copy.65), channel_id=1, source_target_pairs={{0,1},{1,2},{2,3},{4,5},{5,6},{6,7},{8,9},{9,10},{10,11},{12,13},{... | collective-permute-start | bytes 1572872 | tf_op jit(solution)/shard_map/while/body/eval_jaxpr/ppermute | solution.py:18
  199.9 6.6 %collective-permute-done.1 = f32[1,2,256,256]{3,2,1,0:T(8,128)S(1)} collective-permute-done((f32[1,2,256,256]{3,2,1,0:T(8,128)S(1)}, f32[1,2,256,256]{3,2,1,0:T(8,128)S(1)}, u32[]{:S(2)}, u32[]{:S(2)}) %collective-permute-start.1) | collective-permute-done | bytes 524320 | tf_op jit(solution)/shard_map/while/body/eval_jaxpr/ppermute | solution.py:18
  211.6 167.7 %while.50 = (s32[]{:T(128)}, f32[4,1,2,256,256]{4,3,2,1,0:T(8,128)}, f32[1,2,256,256]{3,2,1,0:T(8,128)}, s32[]{:T(128)}, f32[4,1,2,256,256]{4,3,2,1,0:T(8,128)S(...) while((s32[]{:T(128)}, f32[4,1,2,256,256]{4,3,2,1,0:T(8,128)}, ...), condition=%wide.region_7.8_spmd, body=%wide.region_4.7_spmd.sunk | while | flops 2416705536 | bytes 15204615 | solution.py:181
  213.0 29.1 %collective-permute-done = f32[1,2,256,256]{3,2,1,0:T(8,128)S(1)} collective-permute-done((f32[1,2,256,256]{3,2,1,0:T(8,128)}, f32[1,2,256,256]{3,2,1,0:T(8,128)S(1)}, u32[]{:S(2)}, u32[]{:S(2)}) %collective-permute-start) | collective-permute-done | bytes 524320 | tf_op jit(solution)/shard_map/while/body/eval_jaxpr/ppermute | solution.py:18
  244.2 10.0 %collective-permute-done = f32[1,2,256,256]{3,2,1,0:T(8,128)S(1)} collective-permute-done((f32[1,2,256,256]{3,2,1,0:T(8,128)}, f32[1,2,256,256]{3,2,1,0:T(8,128)S(1)}, u32[]{:S(2)}, u32[]{:S(2)}) %collective-permute-start) | collective-permute-done | bytes 524320 | tf_op jit(solution)/shard_map/while/body/eval_jaxpr/ppermute | solution.py:18
  256.3 27.8 %collective-permute-done = f32[1,2,256,256]{3,2,1,0:T(8,128)S(1)} collective-permute-done((f32[1,2,256,256]{3,2,1,0:T(8,128)}, f32[1,2,256,256]{3,2,1,0:T(8,128)S(1)}, u32[]{:S(2)}, u32[]{:S(2)}) %collective-permute-start) | collective-permute-done | bytes 524320 | tf_op jit(solution)/shard_map/while/body/eval_jaxpr/ppermute | solution.py:18
  286.3 27.9 %collective-permute-done = f32[1,2,256,256]{3,2,1,0:T(8,128)S(1)} collective-permute-done((f32[1,2,256,256]{3,2,1,0:T(8,128)}, f32[1,2,256,256]{3,2,1,0:T(8,128)S(1)}, u32[]{:S(2)}, u32[]{:S(2)}) %collective-permute-start) | collective-permute-done | bytes 524320 | tf_op jit(solution)/shard_map/while/body/eval_jaxpr/ppermute | solution.py:18
  314.2 7.8 %conditional.5 = (f32[4,1,2,256,256]{4,3,2,1,0:T(8,128)}, f32[1,2,256,256]{3,2,1,0:T(8,128)}) conditional(s32[]{:T(128)} %convert_element_type.83, f32[4,1,2,256,256]{4,3,2,1,0:T(8,128)} %get-tuple-element.784, (s32[]{:T(128)}, f32[4,1,2,256,256]{4,3,2,1,0:T(8,128)S(1)}, f32[1,2,256,256]{3,2,1,0:T(8,128)S(1)}, f32[4,1,2,256,256]{4,3,2,1,0:T(8,128)}, ...), branch_computations={%region_5.5_spmd, %region_6.6_spmd} | conditional | flops 2416705536 | bytes 13107252 | solution.py:179
  323.3 10.0 %collective-permute-done = f32[1,2,256,256]{3,2,1,0:T(8,128)S(1)} collective-permute-done((f32[1,2,256,256]{3,2,1,0:T(8,128)}, f32[1,2,256,256]{3,2,1,0:T(8,128)S(1)}, u32[]{:S(2)}, u32[]{:S(2)}) %collective-permute-start) | collective-permute-done | bytes 524320 | tf_op jit(solution)/shard_map/while/body/eval_jaxpr/ppermute | solution.py:18
  333.3 7.8 %conditional.5 = (f32[4,1,2,256,256]{4,3,2,1,0:T(8,128)}, f32[1,2,256,256]{3,2,1,0:T(8,128)}) conditional(s32[]{:T(128)} %convert_element_type.83, f32[4,1,2,256,256]{4,3,2,1,0:T(8,128)} %get-tuple-element.784, (s32[]{:T(128)}, f32[4,1,2,256,256]{4,3,2,1,0:T(8,128)S(1)}, f32[1,2,256,256]{3,2,1,0:T(8,128)S(1)}, f32[4,1,2,256,256]{4,3,2,1,0:T(8,128)}, ...), branch_computations={%region_5.5_spmd, %region_6.6_spmd} | conditional | flops 2416705536 | bytes 13107252 | solution.py:179
  342.4 10.0 %collective-permute-done = f32[1,2,256,256]{3,2,1,0:T(8,128)S(1)} collective-permute-done((f32[1,2,256,256]{3,2,1,0:T(8,128)}, f32[1,2,256,256]{3,2,1,0:T(8,128)S(1)}, u32[]{:S(2)}, u32[]{:S(2)}) %collective-permute-start) | collective-permute-done | bytes 524320 | tf_op jit(solution)/shard_map/while/body/eval_jaxpr/ppermute | solution.py:18
  352.4 7.8 %conditional.5 = (f32[4,1,2,256,256]{4,3,2,1,0:T(8,128)}, f32[1,2,256,256]{3,2,1,0:T(8,128)}) conditional(s32[]{:T(128)} %convert_element_type.83, f32[4,1,2,256,256]{4,3,2,1,0:T(8,128)} %get-tuple-element.784, (s32[]{:T(128)}, f32[4,1,2,256,256]{4,3,2,1,0:T(8,128)S(1)}, f32[1,2,256,256]{3,2,1,0:T(8,128)S(1)}, f32[4,1,2,256,256]{4,3,2,1,0:T(8,128)}, ...), branch_computations={%region_5.5_spmd, %region_6.6_spmd} | conditional | flops 2416705536 | bytes 13107252 | solution.py:179
  361.5 10.0 %collective-permute-done = f32[1,2,256,256]{3,2,1,0:T(8,128)S(1)} collective-permute-done((f32[1,2,256,256]{3,2,1,0:T(8,128)}, f32[1,2,256,256]{3,2,1,0:T(8,128)S(1)}, u32[]{:S(2)}, u32[]{:S(2)}) %collective-permute-start) | collective-permute-done | bytes 524320 | tf_op jit(solution)/shard_map/while/body/eval_jaxpr/ppermute | solution.py:18
  371.5 7.8 %conditional.5 = (f32[4,1,2,256,256]{4,3,2,1,0:T(8,128)}, f32[1,2,256,256]{3,2,1,0:T(8,128)}) conditional(s32[]{:T(128)} %convert_element_type.83, f32[4,1,2,256,256]{4,3,2,1,0:T(8,128)} %get-tuple-element.784, (s32[]{:T(128)}, f32[4,1,2,256,256]{4,3,2,1,0:T(8,128)S(1)}, f32[1,2,256,256]{3,2,1,0:T(8,128)S(1)}, f32[4,1,2,256,256]{4,3,2,1,0:T(8,128)}, ...), branch_computations={%region_5.5_spmd, %region_6.6_spmd} | conditional | flops 2416705536 | bytes 13107252 | solution.py:179
  381.2 4.8 %collective-permute-start.3 = (f32[4,1,2,256,256]{4,3,2,1,0:T(8,128)}, f32[4,1,2,256,256]{4,3,2,1,0:T(8,128)S(1)}, u32[]{:S(2)}, u32[]{:S(2)}) collective-permute-start(f32[4,1,2,256,256]{4,3,2,1,0:T(8,128)} %get-tuple-element.547), channel_id=1, source_target_pairs={{4,0},{8,4},{12,8},{16,12},{20,16},{24,20},{28,24},{5,1},{9,5},{13... | collective-permute-start | bytes 6291464 | tf_op jit(solution)/shard_map/ppermute | solution.py:29
  395.2 32.4 %collective-permute-done.2 = f32[4,1,2,256,256]{4,3,2,1,0:T(8,128)} collective-permute-done((f32[4,1,2,256,256]{4,3,2,1,0:T(8,128)}, f32[4,1,2,256,256]{4,3,2,1,0:T(8,128)}, u32[]{:S(2)}, u32[]{:S(2)}) %collective-permute-start.2) | collective-permute-done | bytes 2097184 | tf_op jit(solution)/shard_map/ppermute | solution.py:26
  430.5 5.6 %fusion.63 = f32[4,2,256,256]{3,2,1,0:T(8,128)S(1)} fusion(f32[12,1,2,256,256]{4,3,2,1,0:T(8,128)S(1)} %constant_dynamic-update-slice_fusion, s32[]{:T(128)S(6)} %select_n.68, s32[]{:T(128)S(6)} %select_n.67, s32[]{:T(128)S(6)} %select_n.66, s32[]{:T(128)S(6)} %select_n.65, s32[]{:T(128)S(6)} %select_n.64, s32[]{:T(128)S(6)} %select_n.63, f32[]{:T(128)} %bitcast.63, ...), kind=kOutput, calls=%fused_computation.107 | convolution fusion | flops 1614938112 | bytes 14944292 | tf_op jit(solution)/shard_map/sab,eszbc->eszac/dot_general | solution.py:190
  (243 shorter events, 163.8 us)
Async XLA Ops:
  0.7 3.0 copy-start.3
  0.7 3.1 copy-start.7
  3.9 2.5 copy-start
  7.6 14.7 %collective-permute-start.1 = (f32[1,2,256,256]{3,2,1,0:T(8,128)S(1)}, f32[1,2,256,256]{3,2,1,0:T(8,128)S(1)}, u32[]{:S(2)}, u32[]{:S(2)}) collective-permute-start(f32[1,2,256,256]{3,2,1,0:T(8,128)S(1)} %copy.65), channel_id=1, source_target_pairs={{0,1},{1,2},{2,3},{4,5},{5,6},{6,7},{8,9},{9,10},{10,11},{12,13},{... | collective-permute-start | bytes 1572872 | tf_op jit(solution)/shard_map/while/body/eval_jaxpr/ppermute | solution.py:18
  43.9 11.9 %collective-permute-start.1 = (f32[1,2,256,256]{3,2,1,0:T(8,128)S(1)}, f32[1,2,256,256]{3,2,1,0:T(8,128)S(1)}, u32[]{:S(2)}, u32[]{:S(2)}) collective-permute-start(f32[1,2,256,256]{3,2,1,0:T(8,128)S(1)} %copy.65), channel_id=1, source_target_pairs={{0,1},{1,2},{2,3},{4,5},{5,6},{6,7},{8,9},{9,10},{10,11},{12,13},{... | collective-permute-start | bytes 1572872 | tf_op jit(solution)/shard_map/while/body/eval_jaxpr/ppermute | solution.py:18
  77.3 14.1 %collective-permute-start.1 = (f32[1,2,256,256]{3,2,1,0:T(8,128)S(1)}, f32[1,2,256,256]{3,2,1,0:T(8,128)S(1)}, u32[]{:S(2)}, u32[]{:S(2)}) collective-permute-start(f32[1,2,256,256]{3,2,1,0:T(8,128)S(1)} %copy.65), channel_id=1, source_target_pairs={{0,1},{1,2},{2,3},{4,5},{5,6},{6,7},{8,9},{9,10},{10,11},{12,13},{... | collective-permute-start | bytes 1572872 | tf_op jit(solution)/shard_map/while/body/eval_jaxpr/ppermute | solution.py:18
  113.0 13.3 %collective-permute-start.1 = (f32[1,2,256,256]{3,2,1,0:T(8,128)S(1)}, f32[1,2,256,256]{3,2,1,0:T(8,128)S(1)}, u32[]{:S(2)}, u32[]{:S(2)}) collective-permute-start(f32[1,2,256,256]{3,2,1,0:T(8,128)S(1)} %copy.65), channel_id=1, source_target_pairs={{0,1},{1,2},{2,3},{4,5},{5,6},{6,7},{8,9},{9,10},{10,11},{12,13},{... | collective-permute-start | bytes 1572872 | tf_op jit(solution)/shard_map/while/body/eval_jaxpr/ppermute | solution.py:18
  147.8 12.4 %collective-permute-start.1 = (f32[1,2,256,256]{3,2,1,0:T(8,128)S(1)}, f32[1,2,256,256]{3,2,1,0:T(8,128)S(1)}, u32[]{:S(2)}, u32[]{:S(2)}) collective-permute-start(f32[1,2,256,256]{3,2,1,0:T(8,128)S(1)} %copy.65), channel_id=1, source_target_pairs={{0,1},{1,2},{2,3},{4,5},{5,6},{6,7},{8,9},{9,10},{10,11},{12,13},{... | collective-permute-start | bytes 1572872 | tf_op jit(solution)/shard_map/while/body/eval_jaxpr/ppermute | solution.py:18
  162.3 31.0 %collective-permute-start.1 = (f32[1,2,256,256]{3,2,1,0:T(8,128)S(1)}, f32[1,2,256,256]{3,2,1,0:T(8,128)S(1)}, u32[]{:S(2)}, u32[]{:S(2)}) collective-permute-start(f32[1,2,256,256]{3,2,1,0:T(8,128)S(1)} %copy.65), channel_id=1, source_target_pairs={{0,1},{1,2},{2,3},{4,5},{5,6},{6,7},{8,9},{9,10},{10,11},{12,13},{... | collective-permute-start | bytes 1572872 | tf_op jit(solution)/shard_map/while/body/eval_jaxpr/ppermute | solution.py:18
  195.4 11.1 %collective-permute-start.1 = (f32[1,2,256,256]{3,2,1,0:T(8,128)S(1)}, f32[1,2,256,256]{3,2,1,0:T(8,128)S(1)}, u32[]{:S(2)}, u32[]{:S(2)}) collective-permute-start(f32[1,2,256,256]{3,2,1,0:T(8,128)S(1)} %copy.65), channel_id=1, source_target_pairs={{0,1},{1,2},{2,3},{4,5},{5,6},{6,7},{8,9},{9,10},{10,11},{12,13},{... | collective-permute-start | bytes 1572872 | tf_op jit(solution)/shard_map/while/body/eval_jaxpr/ppermute | solution.py:18
  211.6 174.4 %copy-start.5 = (s32[3]{0:T(128)S(1)}, s32[3]{0:T(128)}, u32[]{:S(2)}) copy-start(s32[3]{0:T(128)} %param.22) | copy-start | bytes 40
  211.6 182.9 %copy-start.6 = (f32[3]{0:T(128)S(1)}, f32[3]{0:T(128)}, u32[]{:S(2)}) copy-start(f32[3]{0:T(128)} %param.23) | copy-start | bytes 40
  211.6 30.5 %collective-permute-start = (f32[1,2,256,256]{3,2,1,0:T(8,128)}, f32[1,2,256,256]{3,2,1,0:T(8,128)S(1)}, u32[]{:S(2)}, u32[]{:S(2)}) collective-permute-start(f32[1,2,256,256]{3,2,1,0:T(8,128)} %get-tuple-element.785), channel_id=1, source_target_pairs={{1,0},{2,1},{3,2},{5,4},{6,5},{7,6},{9,8},{10,9},{11,10},{13,12},{... | collective-permute-start | bytes 1572872 | tf_op jit(solution)/shard_map/while/body/eval_jaxpr/ppermute | solution.py:18
  242.9 11.3 %collective-permute-start = (f32[1,2,256,256]{3,2,1,0:T(8,128)}, f32[1,2,256,256]{3,2,1,0:T(8,128)S(1)}, u32[]{:S(2)}, u32[]{:S(2)}) collective-permute-start(f32[1,2,256,256]{3,2,1,0:T(8,128)} %get-tuple-element.785), channel_id=1, source_target_pairs={{1,0},{2,1},{3,2},{5,4},{6,5},{7,6},{9,8},{10,9},{11,10},{13,12},{... | collective-permute-start | bytes 1572872 | tf_op jit(solution)/shard_map/while/body/eval_jaxpr/ppermute | solution.py:18
  255.0 29.1 %collective-permute-start = (f32[1,2,256,256]{3,2,1,0:T(8,128)}, f32[1,2,256,256]{3,2,1,0:T(8,128)S(1)}, u32[]{:S(2)}, u32[]{:S(2)}) collective-permute-start(f32[1,2,256,256]{3,2,1,0:T(8,128)} %get-tuple-element.785), channel_id=1, source_target_pairs={{1,0},{2,1},{3,2},{5,4},{6,5},{7,6},{9,8},{10,9},{11,10},{13,12},{... | collective-permute-start | bytes 1572872 | tf_op jit(solution)/shard_map/while/body/eval_jaxpr/ppermute | solution.py:18
  285.0 29.2 %collective-permute-start = (f32[1,2,256,256]{3,2,1,0:T(8,128)}, f32[1,2,256,256]{3,2,1,0:T(8,128)S(1)}, u32[]{:S(2)}, u32[]{:S(2)}) collective-permute-start(f32[1,2,256,256]{3,2,1,0:T(8,128)} %get-tuple-element.785), channel_id=1, source_target_pairs={{1,0},{2,1},{3,2},{5,4},{6,5},{7,6},{9,8},{10,9},{11,10},{13,12},{... | collective-permute-start | bytes 1572872 | tf_op jit(solution)/shard_map/while/body/eval_jaxpr/ppermute | solution.py:18
  322.0 11.3 %collective-permute-start = (f32[1,2,256,256]{3,2,1,0:T(8,128)}, f32[1,2,256,256]{3,2,1,0:T(8,128)S(1)}, u32[]{:S(2)}, u32[]{:S(2)}) collective-permute-start(f32[1,2,256,256]{3,2,1,0:T(8,128)} %get-tuple-element.785), channel_id=1, source_target_pairs={{1,0},{2,1},{3,2},{5,4},{6,5},{7,6},{9,8},{10,9},{11,10},{13,12},{... | collective-permute-start | bytes 1572872 | tf_op jit(solution)/shard_map/while/body/eval_jaxpr/ppermute | solution.py:18
  341.1 11.3 %collective-permute-start = (f32[1,2,256,256]{3,2,1,0:T(8,128)}, f32[1,2,256,256]{3,2,1,0:T(8,128)S(1)}, u32[]{:S(2)}, u32[]{:S(2)}) collective-permute-start(f32[1,2,256,256]{3,2,1,0:T(8,128)} %get-tuple-element.785), channel_id=1, source_target_pairs={{1,0},{2,1},{3,2},{5,4},{6,5},{7,6},{9,8},{10,9},{11,10},{13,12},{... | collective-permute-start | bytes 1572872 | tf_op jit(solution)/shard_map/while/body/eval_jaxpr/ppermute | solution.py:18
  360.2 11.3 %collective-permute-start = (f32[1,2,256,256]{3,2,1,0:T(8,128)}, f32[1,2,256,256]{3,2,1,0:T(8,128)S(1)}, u32[]{:S(2)}, u32[]{:S(2)}) collective-permute-start(f32[1,2,256,256]{3,2,1,0:T(8,128)} %get-tuple-element.785), channel_id=1, source_target_pairs={{1,0},{2,1},{3,2},{5,4},{6,5},{7,6},{9,8},{10,9},{11,10},{13,12},{... | collective-permute-start | bytes 1572872 | tf_op jit(solution)/shard_map/while/body/eval_jaxpr/ppermute | solution.py:18
  379.3 48.3 %collective-permute-start.2 = (f32[4,1,2,256,256]{4,3,2,1,0:T(8,128)}, f32[4,1,2,256,256]{4,3,2,1,0:T(8,128)}, u32[]{:S(2)}, u32[]{:S(2)}) collective-permute-start(f32[4,1,2,256,256]{4,3,2,1,0:T(8,128)} %get-tuple-element.547), channel_id=1, source_target_pairs={{0,4},{4,8},{8,12},{12,16},{16,20},{20,24},{24,28},{1,5},{5,9},{9,... | collective-permute-start | bytes 6291464 | tf_op jit(solution)/shard_map/ppermute | solution.py:26
  381.2 48.4 %collective-permute-start.3 = (f32[4,1,2,256,256]{4,3,2,1,0:T(8,128)}, f32[4,1,2,256,256]{4,3,2,1,0:T(8,128)S(1)}, u32[]{:S(2)}, u32[]{:S(2)}) collective-permute-start(f32[4,1,2,256,256]{4,3,2,1,0:T(8,128)} %get-tuple-element.547), channel_id=1, source_target_pairs={{4,0},{8,4},{12,8},{16,12},{20,16},{24,20},{28,24},{5,1},{9,5},{13... | collective-permute-start | bytes 6291464 | tf_op jit(solution)/shard_map/ppermute | solution.py:29
  395.1 34.2 %copy-start.1 = (f32[4,1,2,256,256]{4,3,2,1,0:T(8,128)S(1)}, f32[4,1,2,256,256]{4,3,2,1,0:T(8,128)}, u32[]{:S(2)}) copy-start(f32[4,1,2,256,256]{4,3,2,1,0:T(8,128)} %get-tuple-element.547) | copy-start | bytes 6291460
  429.5 1.0 copy-start.2
  429.6 0.9 copy-start.4
where the time goes:
time: 442 us; the launch traced here: 440 us
  waiting for transfers between devices  219 us (50%)
  matrix products  78.2 us (18%)
  starting transfers between devices  62.2 us (14%)
  local copies, waits for them, and re-layouts  55.4 us (13%)
  other arithmetic  14.9 us (3%)
  between operations  8.69 us (2%)
    ppermute x14, waiting for transfers between devices, passed_along(): lax.ppermute(value, axis, [(source, source + steps) for source in range(i...  186 us
    ppermute x14, starting transfers between devices, passed_along(): lax.ppermute(value, axis, [(source, source + steps) for source in range(i...  55.5 us
    dot_general x96, matrix products, multiply(): return jnp.einsum('...ij,...jk->...ik', left, right, precision=HIGH)  54.4 us
    ppermute x1, waiting for transfers between devices, padded(): lax.ppermute(lax.slice_in_dim(block, block.shape[dim] - width, None, axis...  32.4 us
    dot_general x8, matrix products, times_real(): return jnp.einsum('...ij,jk->...ik', field, matrix, precision=HIGH)  9.91 us
    gather x4, local copies, waits for them, and re-layouts, newton(): real_c = jnp.diagonal(sys_re, axis1=-2, axis2=-1)  9.48 us
    gather x4, local copies, waits for them, and re-layouts, newton(): imag_c = jnp.diagonal(sys_im, axis1=-2, axis2=-1)  9.48 us
  transfers between devices with their start and end apart: 16, of which 15 were waited for; matrix products, arithmetic and copies ran while one was open for 1% of the time, Pallas kernels for 0%

commit v1 on v0

v1 whole, which is shorter than its diff:
```python
import functools

import jax
import jax.numpy as jnp
from jax import lax
from jax.experimental import pallas as pl
from jax.experimental.pallas import tpu as pltpu
from jax.sharding import PartitionSpec as P

NEWTON = 3
ETA = 1.0
CONTACT = 0.6
REACH = 2

F32 = jnp.float32
BF16 = jnp.bfloat16
MESH = pl.DeviceIdType.MESH


def split(value):
    high = value.astype(BF16)
    return high, (value - high.astype(F32)).astype(BF16)


def join(pieces, axis):
    return tuple(jnp.concatenate(parts, axis=axis) for parts in zip(*pieces))


def dot(left, right):
    return jnp.dot(left, right, preferred_element_type=F32)


def matmul(left, right):
    (left_h, left_l), (right_h, right_l) = left, right
    return dot(left_h, right_h) + (dot(left_h, right_l) + dot(left_l, right_h))


def minus(pair):
    return tuple(-part for part in pair)


def complex_product(left, right):
    size = left[0][0].shape[0]
    rows = join(left, 1)
    columns = join([join([right[0], right[1]], 1), join([minus(right[1]), right[0]], 1)], 0)
    result = matmul(rows, columns)
    return result[:, :size], result[:, size:]


def congruence(first, field, second):
    size = first[0].shape[0]
    half = matmul(join(field, 0), second)
    half = join([split(half[:size]), split(half[size:])], 1)
    result = matmul(first, half)
    return result[:, :size], result[:, size:]


def kernel(
    energies, offsets, strength, self_in, onsite, within, between, coupling, groups,
    green, self_out,
    hamil, hops, mats, local, came_f, came_b, sent_b, halo,
    send_f, recv_f, send_b, recv_b, send_h, recv_h,
):
    count, width = self_in.shape[0], self_in.shape[3]
    sections, place = lax.axis_size("section"), lax.axis_index("section")
    spans, seat = lax.axis_size("energy"), lax.axis_index("energy")
    has_prev, has_next = place > 0, place < sections - 1
    has_low, has_high = seat > 0, seat < spans - 1
    last = sections - 1

    barrier = pltpu.get_barrier_semaphore()
    for present, target in (
        (has_prev, {"section": place - 1}),
        (has_next, {"section": place + 1}),
        (has_low, {"energy": seat - 1}),
        (has_high, {"energy": seat + 1}),
    ):
        @pl.when(present)
        def _():
            pl.semaphore_signal(barrier, inc=1, device_id=target, device_id_type=MESH)

    eye = (
        lax.broadcasted_iota(jnp.int32, (width, width), 0)
        == lax.broadcasted_iota(jnp.int32, (width, width), 1)
    )
    hamil[...] = jnp.where(eye, onsite[0:1, :], 0.0) + 0.5 * (within[0] + within[0].T)
    hop = between[0]
    hops[0], hops[1] = split(hop)
    hops[2], hops[3] = split(hop.T)
    row_group = jnp.broadcast_to(groups[0:1, :].astype(F32), (width, width))
    mat = jnp.where(row_group == row_group.T, coupling[0], 0.0)
    mats[0], mats[1] = split(mat)
    mats[2], mats[3] = split(mat.T)

    @pl.when(place == 0)
    def _():
        for index in range(count):
            came_f[index, 0] = jnp.zeros((width, width), F32)
            came_f[index, 1] = jnp.where(eye, -CONTACT, 0.0)

    @pl.when(seat == 0)
    def _():
        halo[0:REACH] = jnp.zeros((REACH, 2, width, width), F32)

    @pl.when(seat == spans - 1)
    def _():
        halo[REACH : 2 * REACH] = jnp.zeros((REACH, 2, width, width), F32)

    peers = sum(present.astype(jnp.int32) for present in (has_prev, has_next, has_low, has_high))
    pl.semaphore_wait(barrier, peers)

    def forward_copy(index):
        return pltpu.make_async_remote_copy(
            src_ref=local.at[index], dst_ref=came_f.at[index],
            send_sem=send_f.at[index], recv_sem=recv_f.at[index],
            device_id={"section": place + 1}, device_id_type=MESH,
        )

    def backward_copy(index):
        return pltpu.make_async_remote_copy(
            src_ref=sent_b.at[index], dst_ref=came_b.at[index],
            send_sem=send_b.at[index], recv_sem=recv_b.at[index],
            device_id={"section": place - 1}, device_id_type=MESH,
        )

    def halo_up(index):
        slot = index - (count - REACH)
        return pltpu.make_async_remote_copy(
            src_ref=green.at[index, 0], dst_ref=halo.at[slot],
            send_sem=send_h.at[slot], recv_sem=recv_h.at[slot],
            device_id={"energy": seat + 1}, device_id_type=MESH,
        )

    def halo_down(index):
        slot = index + REACH
        return pltpu.make_async_remote_copy(
            src_ref=green.at[index, 0], dst_ref=halo.at[slot],
            send_sem=send_h.at[slot], recv_sem=recv_h.at[slot],
            device_id={"energy": seat - 1}, device_id_type=MESH,
        )

    def forward(index):
        @pl.when(has_prev)
        def _():
            forward_copy(index).wait_recv()

        field = (split(came_f[index, 0]), split(came_f[index, 1]))
        left_re, left_im = congruence(
            (hops[2], hops[3]), field, (hops[0], hops[1])
        )
        sys_re = jnp.where(eye, energies[index], 0.0) - hamil[...] - self_in[index, 0, 0] - left_re
        sys_im = jnp.where(eye, ETA, 0.0) - self_in[index, 0, 1] - left_im
        diag_re = jnp.where(eye, sys_re, 0.0)
        diag_im = jnp.where(eye, sys_im, 0.0)
        inverses = []
        for axis in (1, 0):
            real_c = jnp.sum(diag_re, axis=axis, keepdims=True)
            imag_c = jnp.sum(diag_im, axis=axis, keepdims=True)
            modulus = real_c * real_c + imag_c * imag_c
            inverses.append((real_c / modulus, -imag_c / modulus))
        (col_re, col_im), (row_re, row_im) = inverses
        half_re = col_re * sys_re - col_im * sys_im
        half_im = col_re * sys_im + col_im * sys_re
        it_re = jnp.where(eye, 2.0 * col_re, 0.0) - (half_re * row_re - half_im * row_im)
        it_im = jnp.where(eye, 2.0 * col_im, 0.0) - (half_re * row_im + half_im * row_re)
        system = (split(sys_re), split(sys_im))
        for _ in range(NEWTON - 1):
            iterate = (split(it_re), split(it_im))
            mid_re, mid_im = complex_product(system, iterate)
            out_re, out_im = complex_product(iterate, (split(mid_re), split(mid_im)))
            it_re, it_im = 2.0 * it_re - out_re, 2.0 * it_im - out_im
        local[index, 0] = it_re
        local[index, 1] = it_im

        @pl.when(has_next)
        def _():
            forward_copy(index).start()

    def backward(index):
        @pl.when(has_next)
        def _():
            backward_copy(index).wait_recv()
            base_re, base_im = local[index, 0], local[index, 1]
            base = (split(base_re), split(base_im))
            incoming = (split(came_b[index, 0]), split(came_b[index, 1]))
            mid_re, mid_im = complex_product(incoming, base)
            out_re, out_im = complex_product(base, (split(mid_re), split(mid_im)))
            green[index, 0, 0] = base_re + out_re
            green[index, 0, 1] = base_im + out_im

        @pl.when(place == last)
        def _():
            green[index, 0] = local[index]

        @pl.when(has_prev)
        def _():
            field = (split(green[index, 0, 0]), split(green[index, 0, 1]))
            out_re, out_im = congruence((hops[0], hops[1]), field, (hops[2], hops[3]))
            sent_b[index, 0] = out_re
            sent_b[index, 1] = out_im
            backward_copy(index).start()

        @pl.when(has_high & (index >= count - REACH))
        def _():
            halo_up(index).start()

        @pl.when(has_low & (index < REACH))
        def _():
            halo_down(index).start()

    def turn(step, carry):
        ahead = step - place
        back = step - 2 * last + place

        @pl.when((ahead >= 0) & (ahead < count))
        def _():
            forward(ahead)

        @pl.when((back >= 0) & (back < count))
        def _():
            backward(back)

        return carry

    lax.fori_loop(0, count + 2 * last, turn, 0)

    near = jnp.float32(0.0)
    far = jnp.float32(0.0)
    for mode in range(offsets.shape[0]):
        near = near + jnp.where(offsets[mode] == 1, strength[mode], 0.0)
        far = far + jnp.where(offsets[mode] == 2, strength[mode], 0.0)

    @pl.when(has_high)
    def _():
        for slot in range(REACH):
            halo_down(slot).wait_recv()

    def block(index, part):
        if index < 0:
            return halo[index + REACH, part]
        if index >= count:
            return halo[index - count + REACH, part]
        return green[index, 0, part]

    first, second = (mats[0], mats[1]), (mats[2], mats[3])
    waited = [False]
    for index in reversed(range(count)):
        if index < REACH and not waited[0]:
            waited[0] = True

            @pl.when(has_low)
            def _():
                for slot in range(REACH):
                    halo_up(count - REACH + slot).wait_recv()

        field = tuple(
            split(
                near * (block(index - 1, part) + block(index + 1, part))
                + far * (block(index - 2, part) + block(index + 2, part))
            )
            for part in range(2)
        )
        out_re, out_im = congruence(first, field, second)
        self_out[index, 0, 0] = out_re
        self_out[index, 0, 1] = out_im

    @pl.when(has_next)
    def _():
        for index in range(count):
            forward_copy(index).wait_send()

    @pl.when(has_prev)
    def _():
        for index in range(count):
            backward_copy(index).wait_send()

    @pl.when(has_high)
    def _():
        for slot in range(REACH):
            halo_up(count - REACH + slot).wait_send()

    @pl.when(has_low)
    def _():
        for slot in range(REACH):
            halo_down(slot).wait_send()


def per_device(self_in, onsite, within, between, coupling, groups, offsets, strength):
    count, width = self_in.shape[0], self_in.shape[3]
    total = count * lax.axis_size("energy")
    first_index = lax.axis_index("energy") * count
    energies = (
        -1.0
        + (2 * (first_index + jnp.arange(count, dtype=jnp.int32)) + 1).astype(jnp.float32) / total
    )
    smem = pl.BlockSpec(memory_space=pltpu.SMEM)
    vmem = pl.BlockSpec(memory_space=pltpu.VMEM)
    shape = jax.ShapeDtypeStruct(self_in.shape, F32)
    dma = pltpu.SemaphoreType.DMA
    return pl.pallas_call(
        kernel,
        out_shape=(shape, shape),
        in_specs=[smem] * 3 + [vmem] * 6,
        out_specs=(vmem, vmem),
        scratch_shapes=[
            pltpu.VMEM((width, width), F32),
            pltpu.VMEM((4, width, width), BF16),
            pltpu.VMEM((4, width, width), BF16),
            pltpu.VMEM((count, 2, width, width), F32),
            pltpu.VMEM((count, 2, width, width), F32),
            pltpu.VMEM((count, 2, width, width), F32),
            pltpu.VMEM((count, 2, width, width), F32),
            pltpu.VMEM((2 * REACH, 2, width, width), F32),
            dma((count,)), dma((count,)), dma((count,)), dma((count,)),
            dma((2 * REACH,)), dma((2 * REACH,)),
        ],
        compiler_params=pltpu.CompilerParams(
            collective_id=0, has_side_effects=True, vmem_limit_bytes=60 * 2**20
        ),
    )(energies, offsets, strength, self_in, onsite, within, between, coupling, groups)


def solution(mesh):
    placed = (
        P("energy", "section", None, None, None),
        P("section", None),
        P("section", None, None),
        P("section", None, None),
        P("section", None, None),
        P("section", None),
        P(),
        P(),
    )
    return jax.shard_map(
        per_device,
        mesh=mesh,
        in_specs=placed,
        out_specs=(
            P("energy", "section", None, None, None),
            P("energy", "section", None, None, None),
        ),
        check_vma=False,
    )
```

time: 442 us -> 141 us (0.32)
  waiting for transfers between devices: 219 us -> 0 us
  Pallas kernels: 0 us -> 135 us
  matrix products: 78.2 us -> 0 us
  starting transfers between devices: 62.2 us -> 0 us
  local copies, waits for them, and re-layouts: 55.4 us -> 4.52 us
  other arithmetic: 14.9 us -> 0.52 us
  between operations: 8.69 us -> 0.65 us
    ppermute x16 -> x0, waiting for transfers between devices: 219 us -> none  [the longest x14 186 us: passed_along(): lax.ppermute(value, axis, [(source, source + steps) for source in range(i...]
    pallas_call x0 -> x1, Pallas kernels: none -> 135 us  [per_device(): pl.pallas_call(kernel, out_shape=(shape, shape), in_specs=[smem] * 3 + [v...]
    dot_general x114 -> x0, matrix products: 78.2 us -> none  [the longest x96 54.4 us: multiply(): return jnp.einsum('...ij,...jk->...ik', left, right, precision=HIGH)]
    ppermute x16 -> x0, starting transfers between devices: 62.2 us -> none  [the longest x14 55.5 us: passed_along(): lax.ppermute(value, axis, [(source, source + steps) for source in range(i...]
    gather x8 -> x0, local copies, waits for them, and re-layouts: 19 us -> none  [the longest x4 9.48 us: newton(): real_c = jnp.diagonal(sys_re, axis1=-2, axis2=-1)]
    while x8 -> x0, local copies, waits for them, and re-layouts: 10.6 us -> none
    sub x20 -> x0, other arithmetic: 7.63 us -> none  [the longest x8 3.92 us: newton(): iterate = 2.0 * iterate - product(iterate, product(system, iterate))]
    dynamic_update_slice x8 -> x0, other arithmetic: 7.01 us -> none  [the longest x4 3.57 us: forward_work(): lax.dynamic_update_slice_in_dim(locals_all, pieces, start, 0)]
  transfers between devices with their start and end apart: 16 -> 0, of which waited for: 15 -> 0; matrix products, arithmetic and copies ran while one was open for 1% -> 0% of each run, Pallas kernels for 0% -> 0%
where the time goes in v1:
time: 141 us
  Pallas kernels  135 us (96%)
  local copies, waits for them, and re-layouts  4.52 us (3%)
    pallas_call x1, Pallas kernels, per_device(): pl.pallas_call(kernel, out_shape=(shape, shape), in_specs=[smem] * 3 + [v...  135 us
    unnamed x4, local copies, waits for them, and re-layouts  4.52 us

profile of v1, /device:TPU:4, one launch (start us, length us, event | category | flops | bytes accessed | tf_op | source)
XLA Modules:
  0.0 141.0 jit_solution(7580023971369533520)
XLA Ops:
  0.6 0.5 multiply_add_fusion.energies
  1.2 135.3 %shard_map.95 = (f32[4,1,2,256,256]{4,3,2,1,0:T(8,128)}, f32[4,1,2,256,256]{4,3,2,1,0:T(8,128)}) custom-call(f32[4]{0:T(128)} %multiply_add_fusion.energies, s32[3]{0:T(128)} %offsets.1, f32[3]{0:T(128)} %strength.1, f32[4,1,2,256,256]{4,3,2,1,0:T(8,128)} %self_in.1, f32[1,256]{1,0:T(1,128)} %onsite.1, f32[1,256,256]{2,1,0:T(8,128)} %within.1, ...), custom_call_target="tpu_custom_call" | custom-call | tf_op jit(solution)/shard_map/pallas_call | solution.py:300
  136.4 0.0 copy-start
  136.5 3.2 %copy.12 = f32[4,1,2,256,256]{4,3,2,1,0:T(8,128)} copy(f32[4,1,2,256,256]{4,3,2,1,0:T(8,128)} %get-tuple-element.4) | data formatting | bytes 4194304
  139.7 0.0 copy-done
  139.7 1.3 copy.13
Async XLA Ops:
  136.4 3.2 %copy-start = (f32[4,1,2,256,256]{4,3,2,1,0:T(8,128)S(1)}, f32[4,1,2,256,256]{4,3,2,1,0:T(8,128)}, u32[]{:S(2)}) copy-start(f32[4,1,2,256,256]{4,3,2,1,0:T(8,128)} %get-tuple-element.5) | copy-start | bytes 6291460

commit v2 on v1

--- a/solution.py
+++ b/solution.py
@@ -11,6 +11,7 @@
 ETA = 1.0
 CONTACT = 0.6
 REACH = 2
+CHUNKS = 2
 
 F32 = jnp.float32
 BF16 = jnp.bfloat16
@@ -47,6 +48,14 @@
     return result[:, :size], result[:, size:]
 
 
+def complex_columns(block):
+    return join([join([block[0], block[1]], 1), join([minus(block[1]), block[0]], 1)], 0)
+
+
+def rows_of(pair, start, size):
+    return tuple(part[start : start + size] for part in pair)
+
+
 def congruence(first, field, second):
     size = first[0].shape[0]
     half = matmul(join(field, 0), second)
@@ -59,7 +68,7 @@
     energies, offsets, strength, self_in, onsite, within, between, coupling, groups,
     green, self_out,
     hamil, hops, mats, local, came_f, came_b, sent_b, halo,
-    send_f, recv_f, send_b, recv_b, send_h, recv_h,
+    send_f, recv_f, send_b, recv_b, send_h, recv_h, token,
 ):
     count, width = self_in.shape[0], self_in.shape[3]
     sections, place = lax.axis_size("section"), lax.axis_index("section")
@@ -67,6 +76,10 @@
     has_prev, has_next = place > 0, place < sections - 1
     has_low, has_high = seat > 0, seat < spans - 1
     last = sections - 1
+    chunk = width // CHUNKS
+    odd = lax.rem(seat, 2) == 1
+    partner = jnp.where(odd, seat - 1, seat + 1)
+    paced = (place == 0) & has_next & (odd | has_high)
 
     barrier = pltpu.get_barrier_semaphore()
     for present, target in (
@@ -109,17 +122,19 @@
     peers = sum(present.astype(jnp.int32) for present in (has_prev, has_next, has_low, has_high))
     pl.semaphore_wait(barrier, peers)
 
-    def forward_copy(index):
+    def forward_copy(index, piece):
+        rows = pl.ds(piece * chunk, chunk)
         return pltpu.make_async_remote_copy(
-            src_ref=local.at[index], dst_ref=came_f.at[index],
-            send_sem=send_f.at[index], recv_sem=recv_f.at[index],
+            src_ref=local.at[index, :, rows], dst_ref=came_f.at[index, :, rows],
+            send_sem=send_f.at[index, piece], recv_sem=recv_f.at[index, piece],
             device_id={"section": place + 1}, device_id_type=MESH,
         )
 
-    def backward_copy(index):
+    def backward_copy(index, piece):
+        rows = pl.ds(piece * chunk, chunk)
         return pltpu.make_async_remote_copy(
-            src_ref=sent_b.at[index], dst_ref=came_b.at[index],
-            send_sem=send_b.at[index], recv_sem=recv_b.at[index],
+            src_ref=sent_b.at[index, :, rows], dst_ref=came_b.at[index, :, rows],
+            send_sem=send_b.at[index, piece], recv_sem=recv_b.at[index, piece],
             device_id={"section": place - 1}, device_id_type=MESH,
         )
 
@@ -140,14 +155,18 @@
         )
 
     def forward(index):
-        @pl.when(has_prev)
-        def _():
-            forward_copy(index).wait_recv()
-
-        field = (split(came_f[index, 0]), split(came_f[index, 1]))
-        left_re, left_im = congruence(
-            (hops[2], hops[3]), field, (hops[0], hops[1])
-        )
+        halves = []
+        for piece in range(CHUNKS):
+            @pl.when(has_prev)
+            def _():
+                forward_copy(index, piece).wait_recv()
+
+            rows = slice(piece * chunk, (piece + 1) * chunk)
+            field = [split(came_f[index, part, rows]) for part in range(2)]
+            half = matmul(join(field, 0), (hops[0], hops[1]))
+            halves.append(join([split(half[:chunk]), split(half[chunk:])], 1))
+        left = matmul((hops[2], hops[3]), join(halves, 0))
+        left_re, left_im = left[:, :width], left[:, width:]
         sys_re = jnp.where(eye, energies[index], 0.0) - hamil[...] - self_in[index, 0, 0] - left_re
         sys_im = jnp.where(eye, ETA, 0.0) - self_in[index, 0, 1] - left_im
         diag_re = jnp.where(eye, sys_re, 0.0)
@@ -164,27 +183,56 @@
         it_re = jnp.where(eye, 2.0 * col_re, 0.0) - (half_re * row_re - half_im * row_im)
         it_im = jnp.where(eye, 2.0 * col_im, 0.0) - (half_re * row_im + half_im * row_re)
         system = (split(sys_re), split(sys_im))
-        for _ in range(NEWTON - 1):
+        for sweep in range(NEWTON - 1):
             iterate = (split(it_re), split(it_im))
             mid_re, mid_im = complex_product(system, iterate)
-            out_re, out_im = complex_product(iterate, (split(mid_re), split(mid_im)))
-            it_re, it_im = 2.0 * it_re - out_re, 2.0 * it_im - out_im
-        local[index, 0] = it_re
-        local[index, 1] = it_im
-
-        @pl.when(has_next)
-        def _():
-            forward_copy(index).start()
+            columns = complex_columns((split(mid_re), split(mid_im)))
+            if sweep < NEWTON - 2:
+                out = matmul(join(iterate, 1), columns)
+                it_re, it_im = 2.0 * it_re - out[:, :width], 2.0 * it_im - out[:, width:]
+                continue
+            rows_all = join(iterate, 1)
+            for piece in range(CHUNKS):
+                rows = slice(piece * chunk, (piece + 1) * chunk)
+                out = matmul(rows_of(rows_all, piece * chunk, chunk), columns)
+                local[index, 0, rows] = 2.0 * it_re[rows] - out[:, :width]
+                local[index, 1, rows] = 2.0 * it_im[rows] - out[:, width:]
+
+                @pl.when(has_next & jnp.logical_not(paced))
+                def _():
+                    forward_copy(index, piece).start()
+
+        @pl.when(paced)
+        def _():
+            @pl.when(odd | (index > 0))
+            def _():
+                pl.semaphore_wait(token, 1)
+
+            for piece in range(CHUNKS):
+                forward_copy(index, piece).start()
+            for piece in range(CHUNKS - 1):
+                forward_copy(index, piece).wait_send()
+
+            @pl.when(jnp.logical_not(odd) | (index < count - 1))
+            def _():
+                pl.semaphore_signal(
+                    token, inc=1, device_id={"energy": partner}, device_id_type=MESH
+                )
 
     def backward(index):
         @pl.when(has_next)
         def _():
-            backward_copy(index).wait_recv()
             base_re, base_im = local[index, 0], local[index, 1]
             base = (split(base_re), split(base_im))
-            incoming = (split(came_b[index, 0]), split(came_b[index, 1]))
-            mid_re, mid_im = complex_product(incoming, base)
-            out_re, out_im = complex_product(base, (split(mid_re), split(mid_im)))
+            columns = complex_columns(base)
+            mids = []
+            for piece in range(CHUNKS):
+                backward_copy(index, piece).wait_recv()
+                rows = slice(piece * chunk, (piece + 1) * chunk)
+                incoming = join([split(came_b[index, part, rows]) for part in range(2)], 1)
+                mids.append(matmul(incoming, columns))
+            mid = jnp.concatenate(mids, axis=0)
+            out_re, out_im = complex_product(base, (split(mid[:, :width]), split(mid[:, width:])))
             green[index, 0, 0] = base_re + out_re
             green[index, 0, 1] = base_im + out_im
 
@@ -194,11 +242,15 @@
 
         @pl.when(has_prev)
         def _():
-            field = (split(green[index, 0, 0]), split(green[index, 0, 1]))
-            out_re, out_im = congruence((hops[0], hops[1]), field, (hops[2], hops[3]))
-            sent_b[index, 0] = out_re
-            sent_b[index, 1] = out_im
-            backward_copy(index).start()
+            field = join([split(green[index, 0, part]) for part in range(2)], 1)
+            for piece in range(CHUNKS):
+                rows = slice(piece * chunk, (piece + 1) * chunk)
+                half = matmul((hops[0, rows], hops[1, rows]), field)
+                half = join([split(half[:, :width]), split(half[:, width:])], 0)
+                out = matmul(half, (hops[2], hops[3]))
+                sent_b[index, 0, rows] = out[:chunk]
+                sent_b[index, 1, rows] = out[chunk:]
+                backward_copy(index, piece).start()
 
         @pl.when(has_high & (index >= count - REACH))
         def _():
@@ -267,12 +319,18 @@
     @pl.when(has_next)
     def _():
         for index in range(count):
-            forward_copy(index).wait_send()
+            for piece in range(CHUNKS - 1):
+                @pl.when(jnp.logical_not(paced))
+                def _():
+                    forward_copy(index, piece).wait_send()
+
+            forward_copy(index, CHUNKS - 1).wait_send()
 
     @pl.when(has_prev)
     def _():
         for index in range(count):
-            backward_copy(index).wait_send()
+            for piece in range(CHUNKS):
+                backward_copy(index, piece).wait_send()
 
     @pl.when(has_high)
     def _():
@@ -311,8 +369,8 @@
             pltpu.VMEM((count, 2, width, width), F32),
             pltpu.VMEM((count, 2, width, width), F32),
             pltpu.VMEM((2 * REACH, 2, width, width), F32),
-            dma((count,)), dma((count,)), dma((count,)), dma((count,)),
-            dma((2 * REACH,)), dma((2 * REACH,)),
+            dma((count, CHUNKS)), dma((count, CHUNKS)), dma((count, CHUNKS)), dma((count, CHUNKS)),
+            dma((2 * REACH,)), dma((2 * REACH,)), pltpu.SemaphoreType.REGULAR,
         ],
         compiler_params=pltpu.CompilerParams(
             collective_id=0, has_side_effects=True, vmem_limit_bytes=60 * 2**20

time: 141 us -> 143 us (1.014)
  Pallas kernels: 135 us -> 137 us
    pallas_call x1, Pallas kernels: 135 us -> 137 us  [per_device(): pl.pallas_call(kernel, out_shape=(shape, shape), in_specs=[smem] * 3 + [v...]
where the time goes in v2:
time: 143 us
  Pallas kernels  137 us (96%)
  local copies, waits for them, and re-layouts  4.52 us (3%)
    pallas_call x1, Pallas kernels, per_device(): pl.pallas_call(kernel, out_shape=(shape, shape), in_specs=[smem] * 3 + [v...  137 us
    unnamed x4, local copies, waits for them, and re-layouts  4.52 us

profile of v2, /device:TPU:4, one launch (start us, length us, event | category | flops | bytes accessed | tf_op | source)
XLA Modules:
  0.0 142.9 jit_solution(3191917577147429566)
XLA Ops:
  0.6 0.5 multiply_add_fusion.energies
  1.2 137.2 %shard_map.95 = (f32[4,1,2,256,256]{4,3,2,1,0:T(8,128)}, f32[4,1,2,256,256]{4,3,2,1,0:T(8,128)}) custom-call(f32[4]{0:T(128)} %multiply_add_fusion.energies, s32[3]{0:T(128)} %offsets.1, f32[3]{0:T(128)} %strength.1, f32[4,1,2,256,256]{4,3,2,1,0:T(8,128)} %self_in.1, f32[1,256]{1,0:T(1,128)} %onsite.1, f32[1,256,256]{2,1,0:T(8,128)} %within.1, ...), custom_call_target="tpu_custom_call" | custom-call | tf_op jit(solution)/shard_map/pallas_call | solution.py:358
  138.4 0.0 copy-start
  138.4 3.2 %copy.12 = f32[4,1,2,256,256]{4,3,2,1,0:T(8,128)} copy(f32[4,1,2,256,256]{4,3,2,1,0:T(8,128)} %get-tuple-element.4) | data formatting | bytes 4194304
  141.6 0.0 copy-done
  141.6 1.3 copy.13
Async XLA Ops:
  138.4 3.2 %copy-start = (f32[4,1,2,256,256]{4,3,2,1,0:T(8,128)S(1)}, f32[4,1,2,256,256]{4,3,2,1,0:T(8,128)}, u32[]{:S(2)}) copy-start(f32[4,1,2,256,256]{4,3,2,1,0:T(8,128)} %get-tuple-element.5) | copy-start | bytes 6291460

commit v3 on v2

--- a/solution.py
+++ b/solution.py
@@ -68,7 +68,7 @@
     energies, offsets, strength, self_in, onsite, within, between, coupling, groups,
     green, self_out,
     hamil, hops, mats, local, came_f, came_b, sent_b, halo,
-    send_f, recv_f, send_b, recv_b, send_h, recv_h, token,
+    send_f, recv_f, send_b, recv_b, send_h, recv_h,
 ):
     count, width = self_in.shape[0], self_in.shape[3]
     sections, place = lax.axis_size("section"), lax.axis_index("section")
@@ -78,8 +78,6 @@
     last = sections - 1
     chunk = width // CHUNKS
     odd = lax.rem(seat, 2) == 1
-    partner = jnp.where(odd, seat - 1, seat + 1)
-    paced = (place == 0) & has_next & (odd | has_high)
 
     barrier = pltpu.get_barrier_semaphore()
     for present, target in (
@@ -198,26 +196,9 @@
                 local[index, 0, rows] = 2.0 * it_re[rows] - out[:, :width]
                 local[index, 1, rows] = 2.0 * it_im[rows] - out[:, width:]
 
-                @pl.when(has_next & jnp.logical_not(paced))
+                @pl.when(has_next)
                 def _():
                     forward_copy(index, piece).start()
-
-        @pl.when(paced)
-        def _():
-            @pl.when(odd | (index > 0))
-            def _():
-                pl.semaphore_wait(token, 1)
-
-            for piece in range(CHUNKS):
-                forward_copy(index, piece).start()
-            for piece in range(CHUNKS - 1):
-                forward_copy(index, piece).wait_send()
-
-            @pl.when(jnp.logical_not(odd) | (index < count - 1))
-            def _():
-                pl.semaphore_signal(
-                    token, inc=1, device_id={"energy": partner}, device_id_type=MESH
-                )
 
     def backward(index):
         @pl.when(has_next)
@@ -266,11 +247,11 @@
 
         @pl.when((ahead >= 0) & (ahead < count))
         def _():
-            forward(ahead)
+            forward(jnp.where(odd, count - 1 - ahead, ahead))
 
         @pl.when((back >= 0) & (back < count))
         def _():
-            backward(back)
+            backward(jnp.where(odd, count - 1 - back, back))
 
         return carry
 
@@ -319,12 +300,8 @@
     @pl.when(has_next)
     def _():
         for index in range(count):
-            for piece in range(CHUNKS - 1):
-                @pl.when(jnp.logical_not(paced))
-                def _():
-                    forward_copy(index, piece).wait_send()
-
-            forward_copy(index, CHUNKS - 1).wait_send()
+            for piece in range(CHUNKS):
+                forward_copy(index, piece).wait_send()
 
     @pl.when(has_prev)
     def _():
@@ -370,7 +347,7 @@
             pltpu.VMEM((count, 2, width, width), F32),
             pltpu.VMEM((2 * REACH, 2, width, width), F32),
             dma((count, CHUNKS)), dma((count, CHUNKS)), dma((count, CHUNKS)), dma((count, CHUNKS)),
-            dma((2 * REACH,)), dma((2 * REACH,)), pltpu.SemaphoreType.REGULAR,
+            dma((2 * REACH,)), dma((2 * REACH,)),
         ],
         compiler_params=pltpu.CompilerParams(
             collective_id=0, has_side_effects=True, vmem_limit_bytes=60 * 2**20

time: 143 us -> 136 us (0.951)
  Pallas kernels: 137 us -> 129 us
    pallas_call x1, Pallas kernels: 137 us -> 129 us  [per_device(): pl.pallas_call(kernel, out_shape=(shape, shape), in_specs=[smem] * 3 + [v...]
where the time goes in v3:
time: 136 us; the launch traced here: 135 us
  Pallas kernels  129 us (95%)
  local copies, waits for them, and re-layouts  4.52 us (3%)
    pallas_call x1, Pallas kernels, per_device(): pl.pallas_call(kernel, out_shape=(shape, shape), in_specs=[smem] * 3 + [v...  129 us
    unnamed x4, local copies, waits for them, and re-layouts  4.52 us

profile of v3, /device:TPU:4, one launch (start us, length us, event | category | flops | bytes accessed | tf_op | source)
XLA Modules:
  0.0 134.9 jit_solution(3864597545511189223)
XLA Ops:
  0.6 0.5 multiply_add_fusion.energies
  1.2 129.2 %shard_map.95 = (f32[4,1,2,256,256]{4,3,2,1,0:T(8,128)}, f32[4,1,2,256,256]{4,3,2,1,0:T(8,128)}) custom-call(f32[4]{0:T(128)} %multiply_add_fusion.energies, s32[3]{0:T(128)} %offsets.1, f32[3]{0:T(128)} %strength.1, f32[4,1,2,256,256]{4,3,2,1,0:T(8,128)} %self_in.1, f32[1,256]{1,0:T(1,128)} %onsite.1, f32[1,256,256]{2,1,0:T(8,128)} %within.1, ...), custom_call_target="tpu_custom_call" | custom-call | tf_op jit(solution)/shard_map/pallas_call | solution.py:335
  130.4 0.0 copy-start
  130.4 3.2 %copy.12 = f32[4,1,2,256,256]{4,3,2,1,0:T(8,128)} copy(f32[4,1,2,256,256]{4,3,2,1,0:T(8,128)} %get-tuple-element.4) | data formatting | bytes 4194304
  133.6 0.0 copy-done
  133.6 1.3 copy.13
Async XLA Ops:
  130.4 3.2 %copy-start = (f32[4,1,2,256,256]{4,3,2,1,0:T(8,128)S(1)}, f32[4,1,2,256,256]{4,3,2,1,0:T(8,128)}, u32[]{:S(2)}) copy-start(f32[4,1,2,256,256]{4,3,2,1,0:T(8,128)} %get-tuple-element.5) | copy-start | bytes 6291460

commit v4 on v3

--- a/solution.py
+++ b/solution.py
@@ -65,7 +65,7 @@
 
 
 def kernel(
-    energies, offsets, strength, self_in, onsite, within, between, coupling, groups,
+    offsets, strength, self_in, onsite, within, between, coupling, groups,
     green, self_out,
     hamil, hops, mats, local, came_f, came_b, sent_b, halo,
     send_f, recv_f, send_b, recv_b, send_h, recv_h,
@@ -165,7 +165,9 @@
             halves.append(join([split(half[:chunk]), split(half[chunk:])], 1))
         left = matmul((hops[2], hops[3]), join(halves, 0))
         left_re, left_im = left[:, :width], left[:, width:]
-        sys_re = jnp.where(eye, energies[index], 0.0) - hamil[...] - self_in[index, 0, 0] - left_re
+        number = jnp.full((1, width), 2 * (seat * count + index) + 1, jnp.int32)
+        energy = -1.0 + number.astype(F32) / (count * spans)
+        sys_re = jnp.where(eye, energy, 0.0) - hamil[...] - self_in[index, 0, 0] - left_re
         sys_im = jnp.where(eye, ETA, 0.0) - self_in[index, 0, 1] - left_im
         diag_re = jnp.where(eye, sys_re, 0.0)
         diag_im = jnp.where(eye, sys_im, 0.0)
@@ -322,12 +324,6 @@
 
 def per_device(self_in, onsite, within, between, coupling, groups, offsets, strength):
     count, width = self_in.shape[0], self_in.shape[3]
-    total = count * lax.axis_size("energy")
-    first_index = lax.axis_index("energy") * count
-    energies = (
-        -1.0
-        + (2 * (first_index + jnp.arange(count, dtype=jnp.int32)) + 1).astype(jnp.float32) / total
-    )
     smem = pl.BlockSpec(memory_space=pltpu.SMEM)
     vmem = pl.BlockSpec(memory_space=pltpu.VMEM)
     shape = jax.ShapeDtypeStruct(self_in.shape, F32)
@@ -335,7 +331,7 @@
     return pl.pallas_call(
         kernel,
         out_shape=(shape, shape),
-        in_specs=[smem] * 3 + [vmem] * 6,
+        in_specs=[smem] * 2 + [vmem] * 6,
         out_specs=(vmem, vmem),
         scratch_shapes=[
             pltpu.VMEM((width, width), F32),
@@ -352,7 +348,7 @@
         compiler_params=pltpu.CompilerParams(
             collective_id=0, has_side_effects=True, vmem_limit_bytes=60 * 2**20
         ),
-    )(energies, offsets, strength, self_in, onsite, within, between, coupling, groups)
+    )(offsets, strength, self_in, onsite, within, between, coupling, groups)
 
 
 def solution(mesh):

time: 136 us -> 136 us (level)
  no operation moved by 1% of the time
where the time goes in v4:
time: 136 us; the launch traced here: 134 us
  Pallas kernels  129 us (95%)
  local copies, waits for them, and re-layouts  4.52 us (3%)
    pallas_call x1, Pallas kernels, per_device(): pl.pallas_call(kernel, out_shape=(shape, shape), in_specs=[smem] * 2 + [v...  129 us
    unnamed x4, local copies, waits for them, and re-layouts  4.52 us

profile of v4, /device:TPU:4, one launch (start us, length us, event | category | flops | bytes accessed | tf_op | source)
XLA Modules:
  0.0 134.3 jit_solution(282735765818491410)
XLA Ops:
  0.6 129.1 %shard_map.95 = (f32[4,1,2,256,256]{4,3,2,1,0:T(8,128)}, f32[4,1,2,256,256]{4,3,2,1,0:T(8,128)}) custom-call(s32[3]{0:T(128)} %offsets.1, f32[3]{0:T(128)} %strength.1, f32[4,1,2,256,256]{4,3,2,1,0:T(8,128)} %self_in.1, f32[1,256]{1,0:T(1,128)} %onsite.1, f32[1,256,256]{2,1,0:T(8,128)} %within.1, f32[1,256,256]{2,1,0:T(8,128)} %between.1, ...), custom_call_target="tpu_custom_call" | custom-call | tf_op jit(solution)/shard_map/pallas_call | solution.py:331
  129.8 0.0 copy-start
  129.8 3.2 %copy.12 = f32[4,1,2,256,256]{4,3,2,1,0:T(8,128)} copy(f32[4,1,2,256,256]{4,3,2,1,0:T(8,128)} %get-tuple-element.4) | data formatting | bytes 4194304
  133.0 0.0 copy-done
  133.0 1.3 copy.13
Async XLA Ops:
  129.8 3.2 %copy-start = (f32[4,1,2,256,256]{4,3,2,1,0:T(8,128)S(1)}, f32[4,1,2,256,256]{4,3,2,1,0:T(8,128)}, u32[]{:S(2)}) copy-start(f32[4,1,2,256,256]{4,3,2,1,0:T(8,128)} %get-tuple-element.5) | copy-start | bytes 6291460
